TPU v7x, 32 devices: a whole 2x2x4 slice. The times are simulated.
32 devices in a mesh: heads: 4 (over y, core), seq: 8 (over z, x).
Axes of the slice: x: 2, y: 2, z: 4, core: 2. Of those that a mesh axis runs over, the one named last changes fastest.
Arguments:
- queries: bfloat16 [1024, 64, 576], P('seq', 'heads'), may hold values from -6 to 6
- latents: bfloat16 [8, 128, 576], P('seq', 'heads'), may hold values from -6 to 6
- grad_out: bfloat16 [1024, 64, 512], P('seq', 'heads'), may hold values from -6 to 6
- selected: int32 [8, 4], P('seq'), may hold values from 0 to 7, as said below
Outputs:
- output: bfloat16 [1024, 64, 512], P('seq', 'heads')
- grad_query: bfloat16 [1024, 64, 576], P('seq', 'heads')
- latent_grad: float32 [8, 128, 576], P('seq', 'heads')
Inputs may be any that keep to these rules, and one draw needn't show every extreme that they name: `selected`: row i lists 4 different blocks, none of them held on the same index of seq as block i (blocks i and j share it when i // 1 equals j // 1); how often a block is chosen varies widely between blocks.
All inputs are finite; a program needn't handle non-finite values.
Results may differ from a plain program's by a relative error of at most 0.012.
Values may be sent and summed in bfloat16 or wider, within the bound.
A program may use at most 64 MiB of HBM per device.

v0:
```python
import jax
import jax.numpy as jnp
from jax import lax
from jax.sharding import PartitionSpec as P


def shards(queries, latents, grad_out, selected):
    block_count, row_share, key_width = latents.shape
    token_total, head_count, _ = queries.shape
    value_width = grad_out.shape[2]
    key_blocks = selected.shape[1] + 1
    block_size = token_total // block_count
    score_scale = key_width ** (-0.5)
    slices = lax.all_gather(latents, "seq", axis=0, tiled=True)
    list_blocks = slices.shape[0]
    own_blocks = lax.axis_index("seq") * block_count + jnp.arange(block_count, dtype=jnp.int32)
    block_ids = jnp.concatenate([own_blocks[:, None], selected], axis=1).reshape(-1)
    picked = jnp.take(slices, block_ids, axis=0)
    key_row_tiles = lax.all_gather(picked, "heads", axis=1, tiled=True)
    key_row_tiles = key_row_tiles.reshape(block_count, key_blocks * block_size, key_width)
    value_rows = key_row_tiles[:, :, :value_width]
    query_row_tiles = queries.reshape(block_count, block_size, head_count, key_width)
    grad_rows = grad_out.reshape(block_count, block_size, head_count, value_width)
    scores = (
        jnp.einsum(
            "gonv,gmv->gnom", query_row_tiles, key_row_tiles, preferred_element_type=jnp.float32
        )
        * score_scale
    )
    prob_full = jax.nn.softmax(scores, axis=-1)
    prob_half = prob_full.astype(jnp.bfloat16)
    output = jnp.einsum(
        "bhtk,bkl->bthl", prob_half, value_rows, preferred_element_type=jnp.float32
    ).astype(jnp.bfloat16)
    row_delta = jnp.sum(grad_rows.astype(jnp.float32) * output.astype(jnp.float32), axis=-1)
    grad_prob = jnp.einsum(
        "bthl,bkl->bhtk", grad_rows, value_rows, preferred_element_type=jnp.float32
    )
    score_gradient = (
        prob_full * (grad_prob - jnp.transpose(row_delta, (0, 2, 1))[..., None]) * score_scale
    ).astype(jnp.bfloat16)
    grad_query = jnp.einsum(
        "mfgv,mvq->mgfq", score_gradient, key_row_tiles, preferred_element_type=jnp.float32
    ).astype(jnp.bfloat16)
    key_gradient = jnp.einsum(
        "jxnq,jnxa->jqa", score_gradient, query_row_tiles, preferred_element_type=jnp.float32
    )
    grad_value = jnp.einsum(
        "bhtk,bthl->bkl", prob_half, grad_rows, preferred_element_type=jnp.float32
    )
    key_gradient = jnp.concatenate(
        [key_gradient[:, :, :value_width] + grad_value, key_gradient[:, :, value_width:]], axis=-1
    )
    contrib = key_gradient.reshape(block_count * key_blocks, block_size, key_width)
    head_total = lax.psum(contrib, "heads")
    own_share = lax.dynamic_slice_in_dim(
        head_total, lax.axis_index("heads") * row_share, row_share, 1
    )
    one_hot = (jnp.arange(list_blocks, dtype=jnp.int32)[:, None] == block_ids[None, :]).astype(
        jnp.float32
    )
    dense_grad = jnp.dot(
        one_hot,
        own_share.reshape(block_count * key_blocks, row_share * key_width),
        precision=lax.Precision.HIGHEST,
        preferred_element_type=jnp.float32,
    )
    dense_grad = dense_grad.reshape(list_blocks, row_share, key_width)
    holders = list_blocks // block_count
    bundles = dense_grad.reshape(1, holders * block_count, row_share, key_width)
    arrived = lax.all_to_all(bundles, "seq", split_axis=1, concat_axis=0, tiled=True)
    latent_grad = jnp.sum(arrived, axis=0)
    return (
        output.reshape(token_total, head_count, value_width),
        grad_query.reshape(token_total, head_count, key_width),
        latent_grad,
    )


def solution(mesh):
    in_specs = (
        P("seq", "heads", None),
        P("seq", "heads", None),
        P("seq", "heads", None),
        P("seq", None),
    )
    out_specs = (P("seq", "heads", None), P("seq", "heads", None), P("seq", "heads", None))
    return jax.shard_map(shards, mesh=mesh, in_specs=in_specs, out_specs=out_specs, check_vma=False)
```

profile of v0, /device:TPU:0, one launch (start us, length us, event | category | flops | bytes accessed | tf_op | source)
XLA Modules:
  0.0 150.2 jit_solution(12962128840217296627)
XLA Ops:
  7.2 0.0 copy-start
  7.2 0.0 all-reduce.2.cloned.1.call-start
  7.2 0.9 compare_and_fusion
  8.1 32.9 %all_gather.6 = bf16[8,32,576]{2,1,0:T(8,128)(2,1)S(1)} all-gather(bf16[1,32,576]{2,1,0:T(8,128)(2,1)} %param.5), channel_id=1, replica_groups=mesh['heads'=4,'seq'=8] {'seq'}, dimensions={0}, use_global_device_ids=true | all-gather | bytes 331776 | tf_op jit(solution)/shard_map/all_gather | solution.py:14
  41.0 0.6 gather_fusion
  41.6 0.1 broadcast_select_fusion
  41.7 8.8 %all_gather.7 = bf16[5,128,576]{2,1,0:T(8,128)(2,1)S(1)} all-gather(bf16[5,32,576]{2,1,0:T(8,128)(2,1)S(1)} %broadcast_select_fusion), channel_id=1, replica_groups=mesh['heads'=4,'seq'=8] {'heads'}, dimensions={1}, use_global_device_ids=true | all-gather | bytes 921600 | tf_op jit(solution)/shard_map/all_gather | solution.py:19
  50.5 0.0 copy-start.2
  50.5 4.8 %copy.37 = bf16[128,16,512]{0,2,1:T(8,128)(2,1)} copy(bf16[128,16,512]{2,1,0:T(8,128)(2,1)} %param.6) | data formatting | bytes 4194304 | tf_op args[2]
  55.3 0.0 copy-done
  55.3 2.2 %bitcast_reduce_fusion = (f32[16,128]{1,0:T(8,128)S(1)}, f32[640,128,16]{1,0,2:T(8,128)S(1)}) fusion(bf16[640,576,1]{1,0,2:T(8,128)(2,1)S(1)} %bitcast.124, bf16[128,16,576]{0,2,1:T(8,128)(2,1)S(1)} %copy-done), kind=kOutput, calls=%fused_computation.6 | convolution fusion | flops 1512568832 | bytes 8347648 | tf_op jit(solution)/shard_map/gonv,gmv->gnom/dot_general | solution.py:25
  57.5 0.0 copy-start.1
  57.5 0.9 fusion.5
  58.4 0.7 copy-done.1
  59.1 3.5 %fusion.6 = (f32[128,16]{0,1:T(8,128)S(1)}, bf16[512,16,128]{2,0,1:T(8,128)(2,1)}) fusion(bf16[128,16,512]{0,2,1:T(8,128)(2,1)S(1)} %copy-done.1, f32[16,128]{1,0:T(8,128)S(1)} %fusion.5, f32[16,128]{1,0:T(8,128)S(1)} %get-tuple-element.14, f32[640,128,16]{1,0,2:T(8,128)S(1)} %get-tuple-element.15, bf16[1,640,576]{2,1,0:T(8,128)(2,1)S(1)} %bitcast.125), kind=kOutput, calls=%fused_computation.11 | convolution fusion | flops 1352660992 | bytes 10117120 | tf_op jit(solution)/shard_map/bhtk,bkl->bthl/dot_general | solution.py:32
  62.6 0.0 copy-done.2
  62.6 2.0 %fusion.7 = bf16[16,128,640]{1,2,0:T(8,128)(2,1)S(1)} fusion(f32[16,128]{1,0:T(8,128)S(1)} %bitcast.130, f32[16,128]{1,0:T(8,128)S(1)} %fusion.5, f32[16,128]{1,0:T(8,128)S(1)} %get-tuple-element.14, f32[640,128,16]{1,0,2:T(8,128)S(1)} %get-tuple-element.15, bf16[128,16,512]{0,2,1:T(8,128)(2,1)S(1)} %copy-done.1, bf16[1,640,576]{2,1,0:T(8,128)(2,1)S(1)} %bitcast.126), kind=kOutput, calls=%fused_computation.12 | convolution fusion | flops 1351352320 | bytes 10641408 | tf_op jit(solution)/shard_map/bthl,bkl->bhtk/dot_general | solution.py:36
  64.6 0.0 copy-start.3
  64.6 2.0 %convolution_bitcast_fusion = f32[1,640,576]{1,2,0:T(8,128)S(1)} fusion(bf16[16,128,640]{1,2,0:T(8,128)(2,1)S(1)} %fusion.7, bf16[128,16,576]{0,2,1:T(8,128)(2,1)S(1)} %copy-done), kind=kOutput, calls=%fused_computation.21 | convolution fusion | flops 1509949440 | bytes 6455296 | tf_op jit(solution)/shard_map/jxnq,jnxa->jqa/dot_general | solution.py:45
  66.6 0.0 copy-done.3
  66.6 1.9 %fusion.19 = f32[1,640,512]{1,2,0:T(8,128)S(1)} fusion(bf16[128,16,512]{0,2,1:T(8,128)(2,1)S(1)} %copy-done.1, f32[1,640,576]{1,2,0:T(8,128)S(1)} %convolution_bitcast_fusion, f32[16,128]{1,0:T(8,128)S(1)} %fusion.5, f32[16,128]{1,0:T(8,128)S(1)} %get-tuple-element.14, f32[640,128,16]{1,0,2:T(8,128)S(1)} %get-tuple-element.15), kind=kOutput, calls=%fused_computation.23 | convolution fusion | flops 1347747840 | bytes 9977856 | tf_op jit(solution)/shard_map/bhtk,bthl->bkl/dot_general | solution.py:48
  68.6 1.2 pad_maximum_fusion
  69.8 3.0 %copy.43 = f32[1,640,576]{2,1,0:T(8,128)} copy(f32[1,640,576]{1,2,0:T(8,128)} %pad_maximum_fusion) | data formatting | bytes 2949120 | tf_op jit(solution)/shard_map/concatenate | solution.py:51
  72.8 0.0 all-reduce.2.cloned.1.call-update
  72.8 44.1 %all-reduce.2.cloned.1.call-done = f32[5,128,576]{2,1,0:T(8,128)} async-done(((f32[5,128,576]{2,1,0:T(8,128)}), f32[5,128,576]{2,1,0:T(8,128)}) %all-reduce.2.cloned.1.call-update) | async-done | bytes 1474576 | tf_op jit(solution)/shard_map/psum | solution.py:55
  117.0 1.0 constant_dynamic-slice_fusion
  118.0 0.2 reshape.186
  118.2 0.2 dot_general.43
  118.4 0.7 convolution_bitcast_fusion.1
  119.1 1.0 copy.45
  120.0 5.5 %all-to-all-start = ((f32[1,8,32,576]{3,2,0,1:T(8,128)}), f32[1,8,32,576]{3,2,0,1:T(8,128)S(1)}, u32[]{:S(2)}, u32[]{:S(2)}) async-start(f32[1,8,32,576]{3,2,0,1:T(8,128)} %copy.45), calls=%async_computation | async-start | bytes 1310720 | tf_op jit(solution)/shard_map/all_to_all | solution.py:71
  125.5 4.5 %copy.46 = bf16[128,16,512]{2,1,0:T(8,128)(2,1)} copy(bf16[128,16,512]{0,2,1:T(8,128)(2,1)} %bitcast.123) | data formatting | bytes 4194304
  130.1 5.4 %convert_bitcast_fusion = bf16[128,16,576]{0,2,1:T(8,128)(2,1)} fusion(bf16[640,576,1]{1,0,2:T(8,128)(2,1)} %bitcast.127, bf16[16,128,640]{1,2,0:T(8,128)(2,1)} %copy-done.3), kind=kOutput, calls=%fused_computation.18 | convolution fusion | flops 1511129088 | bytes 5718016 | tf_op jit(solution)/shard_map/mfgv,mvq->mgfq/dot_general | solution.py:42
  135.5 7.2 %all-to-all-done = f32[1,8,32,576]{3,2,0,1:T(8,128)S(1)} async-done(((f32[1,8,32,576]{3,2,0,1:T(8,128)}), f32[1,8,32,576]{3,2,0,1:T(8,128)S(1)}, u32[]{:S(2)}, u32[]{:S(2)}) %all-to-all-start) | async-done | bytes 589856 | tf_op jit(solution)/shard_map/all_to_all | solution.py:71
  142.7 0.7 reduce_sum.34
  (3 shorter events, 0.0 us)
Async XLA Ops:
  7.2 48.1 %copy-start = (bf16[128,16,576]{0,2,1:T(8,128)(2,1)S(1)}, bf16[128,16,576]{0,2,1:T(8,128)(2,1)}, u32[]{:S(2)}) copy-start(bf16[128,16,576]{0,2,1:T(8,128)(2,1)} %param.4) | copy-start | bytes 7077892
  7.2 109.8 %all-reduce.2.cloned.1.call-start = ((), (), s32[]{:S(2)}) async-start(), calls=%async_computation.1 | async-start | bytes 3276800 | tf_op jit(solution)/shard_map/psum | solution.py:55
  50.5 12.1 %copy-start.2 = (bf16[5,128,576]{2,1,0:T(8,128)(2,1)}, bf16[5,128,576]{2,1,0:T(8,128)(2,1)S(1)}, u32[]{:S(2)}) copy-start(bf16[5,128,576]{2,1,0:T(8,128)(2,1)S(1)} %all_gather.7) | copy-start | bytes 2211844
  57.5 1.6 %copy-start.1 = (bf16[128,16,512]{0,2,1:T(8,128)(2,1)S(1)}, bf16[128,16,512]{0,2,1:T(8,128)(2,1)}, u32[]{:S(2)}) copy-start(bf16[128,16,512]{0,2,1:T(8,128)(2,1)} %copy.37) | copy-start | bytes 6291460
  64.6 2.0 %copy-start.3 = (bf16[16,128,640]{1,2,0:T(8,128)(2,1)}, bf16[16,128,640]{1,2,0:T(8,128)(2,1)S(1)}, u32[]{:S(2)}) copy-start(bf16[16,128,640]{1,2,0:T(8,128)(2,1)S(1)} %fusion.7) | copy-start | bytes 7864324
  120.0 22.7 %all-to-all-start = ((f32[1,8,32,576]{3,2,0,1:T(8,128)}), f32[1,8,32,576]{3,2,0,1:T(8,128)S(1)}, u32[]{:S(2)}, u32[]{:S(2)}) async-start(f32[1,8,32,576]{3,2,0,1:T(8,128)} %copy.45), calls=%async_computation | async-start | bytes 1310720 | tf_op jit(solution)/shard_map/all_to_all | solution.py:71
Sparse Core Ops, SparseCore 0:
  73.0 43.9 all-reduce.1
where the time goes:
time: 151 us; the launch traced here: 150 us
  waiting for transfers between devices  51.3 us (34%)
  blocking collectives  41.7 us (28%)
  matrix products  17.7 us (12%)
  local copies, waits for them, and re-layouts  16.1 us (11%)
  between operations  14.1 us (9%)
  starting transfers between devices  5.55 us (4%)
  other arithmetic  3.74 us (2%)
    psum x1, waiting for transfers between devices, shards(): head_total = lax.psum(contrib, 'heads')  44.1 us
    all_gather x1, blocking collectives, shards(): slices = lax.all_gather(latents, 'seq', axis=0, tiled=True)  32.9 us
    unnamed x10, local copies, waits for them, and re-layouts  10 us
    all_gather x1, blocking collectives, shards(): key_row_tiles = lax.all_gather(picked, 'heads', axis=1, tiled=True)  8.8 us
    all_to_all x1, waiting for transfers between devices, shards(): lax.all_to_all(bundles, 'seq', split_axis=1, concat_axis=0, tiled=True)  7.21 us
    all_to_all x1, starting transfers between devices, shards(): lax.all_to_all(bundles, 'seq', split_axis=1, concat_axis=0, tiled=True)  5.51 us
    dot_general x1, matrix products, shards(): jnp.einsum('mfgv,mvq->mgfq', score_gradient, key_row_tiles, preferred_ele...  5.43 us
    dot_general x1, matrix products, shards(): jnp.einsum('bhtk,bkl->bthl', prob_half, value_rows, preferred_element_typ...  3.47 us
  transfers between devices with their start and end apart: 2, of which 2 were waited for; matrix products, arithmetic and copies ran while one was open for 7% of the time, Pallas kernels for 0%

commit v1 on v0

--- a/solution.py
+++ b/solution.py
@@ -52,7 +52,13 @@
         [key_gradient[:, :, :value_width] + grad_value, key_gradient[:, :, value_width:]], axis=-1
     )
     contrib = key_gradient.reshape(block_count * key_blocks, block_size, key_width)
-    head_total = lax.psum(contrib, "heads")
+    devices = lax.axis_size("heads")
+    head_total, reach = (contrib, 1)
+    while reach < devices:
+        head_total = head_total + lax.ppermute(
+            head_total, "heads", [(i, i ^ reach) for i in range(devices)]
+        )
+        reach = 2 * reach
     own_share = lax.dynamic_slice_in_dim(
         head_total, lax.axis_index("heads") * row_share, row_share, 1
     )

time: 151 us -> 142 us (0.940)
  between operations: 14.1 us -> 0.75 us
  waiting for transfers between devices: 51.3 us -> 44.5 us
  other arithmetic: 3.74 us -> 10.2 us
  local copies, waits for them, and re-layouts: 16.1 us -> 19.9 us
    psum x1 -> x0, waiting for transfers between devices: 44.1 us -> none  [shards(): head_total = lax.psum(contrib, 'heads')]
    ppermute x0 -> x2, waiting for transfers between devices: none -> 37.5 us  [shards(): lax.ppermute(head_total, 'heads', [(i, i ^ reach) for i in range(devices)])]
    add x0 -> x2, other arithmetic: none -> 6.44 us  [shards(): head_total + lax.ppermute(head_total, 'heads', [(i, i ^ reach) for i in r...]
    reshape x0 -> x1, local copies, waits for them, and re-layouts: none -> 3.03 us  [shards(): key_gradient.reshape(block_count * key_blocks, block_size, key_width)]
  transfers between devices with their start and end apart: 2 -> 3, of which waited for: 2 -> 3; matrix products, arithmetic and copies ran while one was open for 7% -> 7% of each run, Pallas kernels for 0% -> 0%
where the time goes in v1:
time: 142 us; the launch traced here: 141 us
  waiting for transfers between devices  44.5 us (31%)
  blocking collectives  41.7 us (29%)
  local copies, waits for them, and re-layouts  19.9 us (14%)
  matrix products  17.9 us (13%)
  other arithmetic  10.2 us (7%)
  starting transfers between devices  6.41 us (5%)
    ppermute x2, waiting for transfers between devices, shards(): lax.ppermute(head_total, 'heads', [(i, i ^ reach) for i in range(devices)])  37.5 us
    all_gather x1, blocking collectives, shards(): slices = lax.all_gather(latents, 'seq', axis=0, tiled=True)  32.9 us
    unnamed x10, local copies, waits for them, and re-layouts  10 us
    all_gather x1, blocking collectives, shards(): key_row_tiles = lax.all_gather(picked, 'heads', axis=1, tiled=True)  8.8 us
    all_to_all x1, waiting for transfers between devices, shards(): lax.all_to_all(bundles, 'seq', split_axis=1, concat_axis=0, tiled=True)  7 us
    add x2, other arithmetic, shards(): head_total + lax.ppermute(head_total, 'heads', [(i, i ^ reach) for i in r...  6.44 us
    all_to_all x1, starting transfers between devices, shards(): lax.all_to_all(bundles, 'seq', split_axis=1, concat_axis=0, tiled=True)  5.55 us
    dot_general x1, matrix products, shards(): jnp.einsum('mfgv,mvq->mgfq', score_gradient, key_row_tiles, preferred_ele...  5.43 us
  transfers between devices with their start and end apart: 3, of which 3 were waited for; matrix products, arithmetic and copies ran while one was open for 7% of the time, Pallas kernels for 0%

profile of v1, /device:TPU:0, one launch (start us, length us, event | category | flops | bytes accessed | tf_op | source)
XLA Modules:
  0.0 141.3 jit_solution(11885411975190001142)
XLA Ops:
  0.6 0.0 copy-start
  0.6 0.9 compare_and_fusion
  1.5 32.9 %all_gather.6 = bf16[8,32,576]{2,1,0:T(8,128)(2,1)S(1)} all-gather(bf16[1,32,576]{2,1,0:T(8,128)(2,1)} %param.5), channel_id=1, replica_groups=mesh['heads'=4,'seq'=8] {'seq'}, dimensions={0}, use_global_device_ids=true | all-gather | bytes 331776 | tf_op jit(solution)/shard_map/all_gather | solution.py:14
  34.4 0.6 gather_fusion
  35.0 0.1 broadcast_select_fusion
  35.1 8.8 %all_gather.7 = bf16[5,128,576]{2,1,0:T(8,128)(2,1)S(1)} all-gather(bf16[5,32,576]{2,1,0:T(8,128)(2,1)S(1)} %broadcast_select_fusion), channel_id=1, replica_groups=mesh['heads'=4,'seq'=8] {'heads'}, dimensions={1}, use_global_device_ids=true | all-gather | bytes 921600 | tf_op jit(solution)/shard_map/all_gather | solution.py:19
  43.9 0.0 copy-start.2
  43.9 4.8 %copy.56 = bf16[128,16,512]{0,2,1:T(8,128)(2,1)} copy(bf16[128,16,512]{2,1,0:T(8,128)(2,1)} %param.6) | data formatting | bytes 4194304 | tf_op args[2]
  48.7 0.0 copy-done
  48.7 2.2 %bitcast_reduce_fusion = (f32[16,128]{1,0:T(8,128)S(1)}, f32[640,128,16]{1,0,2:T(8,128)S(1)}) fusion(bf16[640,576,1]{1,0,2:T(8,128)(2,1)S(1)} %bitcast.124, bf16[128,16,576]{0,2,1:T(8,128)(2,1)S(1)} %copy-done), kind=kOutput, calls=%fused_computation.6 | convolution fusion | flops 1512568832 | bytes 8347648 | tf_op jit(solution)/shard_map/gonv,gmv->gnom/dot_general | solution.py:25
  50.9 0.0 copy-start.1
  50.9 0.9 fusion.5
  51.8 0.7 copy-done.1
  52.5 3.5 %fusion.6 = (f32[128,16]{0,1:T(8,128)S(1)}, bf16[512,16,128]{2,0,1:T(8,128)(2,1)}) fusion(bf16[128,16,512]{0,2,1:T(8,128)(2,1)S(1)} %copy-done.1, f32[16,128]{1,0:T(8,128)S(1)} %fusion.5, f32[16,128]{1,0:T(8,128)S(1)} %get-tuple-element.17, f32[640,128,16]{1,0,2:T(8,128)S(1)} %get-tuple-element.18, bf16[1,640,576]{2,1,0:T(8,128)(2,1)S(1)} %bitcast.125), kind=kOutput, calls=%fused_computation.11 | convolution fusion | flops 1352660992 | bytes 10117120 | tf_op jit(solution)/shard_map/bhtk,bkl->bthl/dot_general | solution.py:32
  56.0 0.0 copy-done.2
  56.0 2.2 %fusion.7 = bf16[16,128,640]{1,2,0:T(8,128)(2,1)S(1)} fusion(f32[16,128]{1,0:T(8,128)S(1)} %bitcast.130, f32[16,128]{1,0:T(8,128)S(1)} %fusion.5, f32[16,128]{1,0:T(8,128)S(1)} %get-tuple-element.17, f32[640,128,16]{1,0,2:T(8,128)S(1)} %get-tuple-element.18, bf16[128,16,512]{0,2,1:T(8,128)(2,1)S(1)} %copy-done.1, bf16[1,640,576]{2,1,0:T(8,128)(2,1)S(1)} %bitcast.126), kind=kOutput, calls=%fused_computation.12 | convolution fusion | flops 1351352320 | bytes 10641408 | tf_op jit(solution)/shard_map/bthl,bkl->bhtk/dot_general | solution.py:36
  58.2 0.0 copy-start.3
  58.2 2.0 %convolution_bitcast_fusion = f32[1,640,576]{1,2,0:T(8,128)S(1)} fusion(bf16[16,128,640]{1,2,0:T(8,128)(2,1)S(1)} %fusion.7, bf16[128,16,576]{0,2,1:T(8,128)(2,1)S(1)} %copy-done), kind=kOutput, calls=%fused_computation.22 | convolution fusion | flops 1509949440 | bytes 6455296 | tf_op jit(solution)/shard_map/jxnq,jnxa->jqa/dot_general | solution.py:45
  60.2 0.0 copy-done.3
  60.2 1.9 %fusion.19 = f32[1,640,512]{1,2,0:T(8,128)S(1)} fusion(bf16[128,16,512]{0,2,1:T(8,128)(2,1)S(1)} %copy-done.1, f32[1,640,576]{1,2,0:T(8,128)S(1)} %convolution_bitcast_fusion, f32[16,128]{1,0:T(8,128)S(1)} %fusion.5, f32[16,128]{1,0:T(8,128)S(1)} %get-tuple-element.17, f32[640,128,16]{1,0,2:T(8,128)S(1)} %get-tuple-element.18), kind=kOutput, calls=%fused_computation.24 | convolution fusion | flops 1347747840 | bytes 9977856 | tf_op jit(solution)/shard_map/bhtk,bthl->bkl/dot_general | solution.py:48
  62.2 1.2 pad_maximum_fusion
  63.4 3.0 %copy.62 = f32[1,640,576]{2,1,0:T(8,128)} copy(f32[1,640,576]{1,2,0:T(8,128)} %pad_maximum_fusion) | data formatting | bytes 2949120 | tf_op jit(solution)/shard_map/concatenate | solution.py:51
  66.4 3.0 %copy.64 = f32[5,128,576]{1,2,0:T(8,128)} copy(f32[5,128,576]{2,1,0:T(8,128)} %bitcast.121) | data formatting | bytes 2949120 | tf_op jit(solution)/shard_map/reshape | solution.py:54
  69.4 0.3 collective-permute-start
  69.8 3.1 %collective-permute-done = f32[5,128,576]{1,2,0:T(8,128)S(1)} collective-permute-done((f32[5,128,576]{1,2,0:T(8,128)}, f32[5,128,576]{1,2,0:T(8,128)S(1)}, u32[]{:S(2)}, u32[]{:S(2)}) %collective-permute-start) | collective-permute-done | bytes 1474592 | tf_op jit(solution)/shard_map/ppermute | solution.py:58
  72.9 2.7 %add.30 = f32[5,128,576]{1,2,0:T(8,128)} add(f32[5,128,576]{1,2,0:T(8,128)} %copy.64, f32[5,128,576]{1,2,0:T(8,128)S(1)} %collective-permute-done) | non-fusion elementwise | flops 368640 | bytes 4423680 | tf_op jit(solution)/shard_map/add | solution.py:58
  75.6 0.5 collective-permute-start.1
  76.1 34.4 %collective-permute-done.1 = f32[5,128,576]{1,2,0:T(8,128)} collective-permute-done((f32[5,128,576]{1,2,0:T(8,128)}, f32[5,128,576]{1,2,0:T(8,128)}, u32[]{:S(2)}, u32[]{:S(2)}) %collective-permute-start.1) | collective-permute-done | bytes 1474592 | tf_op jit(solution)/shard_map/ppermute | solution.py:58
  110.5 3.7 %dynamic-slice_add_fusion = f32[5,32,576]{1,2,0:T(8,128)} fusion(f32[5,128,576]{1,2,0:T(8,128)} %collective-permute-done.1, s32[]{:T(128)S(6)} %select_n.26, f32[5,128,576]{1,2,0:T(8,128)} %add.30), kind=kLoop, calls=%fused_computation.20 | loop fusion | flops 92160 | bytes 1105924 | tf_op jit(solution)/shard_map/add | solution.py:58
  114.2 1.8 %copy.65 = f32[5,32,576]{2,1,0:T(8,128)S(1)} copy(f32[5,32,576]{1,2,0:T(8,128)} %dynamic-slice_add_fusion) | data formatting | bytes 737280 | tf_op jit(solution)/shard_map/dynamic_slice | solution.py:62
  116.0 0.2 reshape.186
  116.3 0.2 dot_general.43
  116.5 0.7 convolution_bitcast_fusion.1
  117.1 1.0 copy.67
  118.1 5.6 %all-to-all-start = ((f32[1,8,32,576]{3,2,0,1:T(8,128)}), f32[1,8,32,576]{3,2,0,1:T(8,128)S(1)}, u32[]{:S(2)}, u32[]{:S(2)}) async-start(f32[1,8,32,576]{3,2,0,1:T(8,128)} %copy.67), calls=%async_computation | async-start | bytes 1310720 | tf_op jit(solution)/shard_map/all_to_all | solution.py:77
  123.7 4.5 %copy.68 = bf16[128,16,512]{2,1,0:T(8,128)(2,1)} copy(bf16[128,16,512]{0,2,1:T(8,128)(2,1)} %bitcast.123) | data formatting | bytes 4194304
  128.2 5.4 %convert_bitcast_fusion = bf16[128,16,576]{0,2,1:T(8,128)(2,1)} fusion(bf16[640,576,1]{1,0,2:T(8,128)(2,1)} %bitcast.127, bf16[16,128,640]{1,2,0:T(8,128)(2,1)} %copy-done.3), kind=kOutput, calls=%fused_computation.18 | convolution fusion | flops 1511129088 | bytes 5718016 | tf_op jit(solution)/shard_map/mfgv,mvq->mgfq/dot_general | solution.py:42
  133.6 7.0 %all-to-all-done = f32[1,8,32,576]{3,2,0,1:T(8,128)S(1)} async-done(((f32[1,8,32,576]{3,2,0,1:T(8,128)}), f32[1,8,32,576]{3,2,0,1:T(8,128)S(1)}, u32[]{:S(2)}, u32[]{:S(2)}) %all-to-all-start) | async-done | bytes 589856 | tf_op jit(solution)/shard_map/all_to_all | solution.py:77
  140.6 0.7 reduce_sum.34
  (3 shorter events, 0.0 us)
Async XLA Ops:
  0.6 48.1 %copy-start = (bf16[128,16,576]{0,2,1:T(8,128)(2,1)S(1)}, bf16[128,16,576]{0,2,1:T(8,128)(2,1)}, u32[]{:S(2)}) copy-start(bf16[128,16,576]{0,2,1:T(8,128)(2,1)} %param.4) | copy-start | bytes 7077892
  43.9 12.1 %copy-start.2 = (bf16[5,128,576]{2,1,0:T(8,128)(2,1)}, bf16[5,128,576]{2,1,0:T(8,128)(2,1)S(1)}, u32[]{:S(2)}) copy-start(bf16[5,128,576]{2,1,0:T(8,128)(2,1)S(1)} %all_gather.7) | copy-start | bytes 2211844
  50.9 1.6 %copy-start.1 = (bf16[128,16,512]{0,2,1:T(8,128)(2,1)S(1)}, bf16[128,16,512]{0,2,1:T(8,128)(2,1)}, u32[]{:S(2)}) copy-start(bf16[128,16,512]{0,2,1:T(8,128)(2,1)} %copy.56) | copy-start | bytes 6291460
  58.2 2.0 %copy-start.3 = (bf16[16,128,640]{1,2,0:T(8,128)(2,1)}, bf16[16,128,640]{1,2,0:T(8,128)(2,1)S(1)}, u32[]{:S(2)}) copy-start(bf16[16,128,640]{1,2,0:T(8,128)(2,1)S(1)} %fusion.7) | copy-start | bytes 7864324
  69.4 3.5 %collective-permute-start = (f32[5,128,576]{1,2,0:T(8,128)}, f32[5,128,576]{1,2,0:T(8,128)S(1)}, u32[]{:S(2)}, u32[]{:S(2)}) collective-permute-start(f32[5,128,576]{1,2,0:T(8,128)} %copy.64), channel_id=1, source_target_pairs={{0,8},{8,0},{16,24},{24,16},{1,9},{9,1},{17,25},{25,17},{2,10},{10... | collective-permute-start | bytes 4423688 | tf_op jit(solution)/shard_map/ppermute | solution.py:58
  75.6 34.9 %collective-permute-start.1 = (f32[5,128,576]{1,2,0:T(8,128)}, f32[5,128,576]{1,2,0:T(8,128)}, u32[]{:S(2)}, u32[]{:S(2)}) collective-permute-start(f32[5,128,576]{1,2,0:T(8,128)} %add.30), channel_id=1, source_target_pairs={{0,16},{8,24},{16,0},{24,8},{1,17},{9,25},{17,1},{25,9},{2,18},{10... | collective-permute-start | bytes 4423688 | tf_op jit(solution)/shard_map/ppermute | solution.py:58
  118.1 22.5 %all-to-all-start = ((f32[1,8,32,576]{3,2,0,1:T(8,128)}), f32[1,8,32,576]{3,2,0,1:T(8,128)S(1)}, u32[]{:S(2)}, u32[]{:S(2)}) async-start(f32[1,8,32,576]{3,2,0,1:T(8,128)} %copy.67), calls=%async_computation | async-start | bytes 1310720 | tf_op jit(solution)/shard_map/all_to_all | solution.py:77
